TPU v7x, 512 devices: a whole 4x4x16 slice. The times are simulated.
512 devices in a mesh: lon: 16 (over z), lat: 8 (over x_lo, y), ch: 4 (over x_hi, core).
Axes of the slice: x: 4 (x_hi: 2, x_lo: 2; x = x_hi * 2 + x_lo), y: 4, z: 16, core: 2. Of those that a mesh axis runs over, the one named last changes fastest.
Arguments:
- ocean_state: bfloat16 [300, 256, 2048], P('ch', 'lat', 'lon'), may hold values from -6 to 6
- land_mask: int32 [256, 2048], P('lat', 'lon'), may hold values 0 or 1
- out_grad: bfloat16 [300, 256, 2048], P('ch', 'lat', 'lon'), may hold values from -6 to 6
- swath_offset: int32 [8, 16, 512], P('lat', 'lon'), may hold values from 0 to 4095
- swath_value: float32 [8, 16, 512], P('lat', 'lon'), may hold values from -8 to 8
- depth_kernel: float32 [3, 3, 300], P(None, None, 'ch'), may hold values from -2.5 to 2.5
- expand_weight: bfloat16 [300, 600], P(None, 'ch'), may hold values from -0.375 to 0.375
- expand_bias: float32 [600], P('ch'), may hold values from -3 to 3
- project_weight: bfloat16 [600, 300], P('ch'), may hold values from -0.25 to 0.25
Outputs:
- state_grad: bfloat16 [300, 256, 2048], P('ch', 'lat', 'lon')
- expand_grad: float32 [300, 600], P(None, 'ch')
- project_grad: float32 [600, 300], P('ch')
- bias_grad: float32 [600], P('ch')
- kernel_grad: float32 [3, 3, 300], P(None, None, 'ch')
Inputs may be any that keep to these rules, and one draw needn't show every extreme that they name: `swath_offset`: position of a swath point in row-major order over the 32 x 128 cells of its device's block.
All inputs are finite; a program needn't handle non-finite values. No bound on the sum of `land_mask` on one device may be relied on, other than what follows from the above.
Results may differ from a plain program's by a relative error of at most 0.014.
Values may be sent and summed in bfloat16 or wider, within the bound.
A program may use at most 64 MiB of HBM per device.

v0:
```python
import math
import jax
import jax.numpy as jnp
from jax import lax
from jax.sharding import PartitionSpec as P

DILATION_STEP = 2


def with_halo(block, sides, width):
    for axis, dim in sides:
        count = lax.axis_size(axis)
        forward = [(i, i + 1) for i in range(count - 1)]
        forward.append((count - 1, 0))
        backward = [(target, source) for source, target in forward]
        low = lax.ppermute(
            lax.slice_in_dim(block, block.shape[dim] - width, None, axis=dim), axis, forward
        )
        high = lax.ppermute(lax.slice_in_dim(block, 0, width, axis=dim), axis, backward)
        block = jnp.concatenate([low, block, high], axis=dim)
    return block


def extend(ocean_field):
    count_of_rows = ocean_field.shape[1]
    column_count = ocean_field.shape[2]
    halo_padded = with_halo(ocean_field, (("lon", 2), ("lat", 1)), DILATION_STEP)
    uppermost_rows = ocean_field[:, count_of_rows - DILATION_STEP :, :]
    gathered = lax.all_gather(uppermost_rows, "lon", axis=2, tiled=True)
    seam_mirrored = gathered[:, ::-1, ::-1]
    seam_mirrored = jnp.concatenate(
        [seam_mirrored[:, :, -DILATION_STEP:], seam_mirrored, seam_mirrored[:, :, :DILATION_STEP]],
        axis=2,
    )
    northern_border = lax.dynamic_slice_in_dim(
        seam_mirrored, lax.axis_index("lon") * column_count, column_count + 2 * DILATION_STEP, 2
    )
    latitude_index = lax.axis_index("lat")
    southern_boundary = halo_padded[:, :DILATION_STEP, :]
    southern_border = jnp.where(
        latitude_index == 0, jnp.zeros_like(southern_boundary), southern_boundary
    )
    northern_border = jnp.where(
        latitude_index == lax.axis_size("lat") - 1,
        northern_border,
        halo_padded[:, count_of_rows + DILATION_STEP :, :],
    )
    return jnp.concatenate(
        [
            southern_border,
            halo_padded[:, DILATION_STEP : count_of_rows + DILATION_STEP, :],
            northern_border,
        ],
        axis=1,
    )


def on_device(
    ocean_state,
    land_mask,
    out_grad,
    swath_offset,
    swath_value,
    depth_kernel,
    expand_weight,
    expand_bias,
    project_weight,
):
    channels_per_shard = ocean_state.shape[0]
    count_of_rows = ocean_state.shape[1]
    column_count = ocean_state.shape[2]
    cells = count_of_rows * column_count
    scale = 1.0 / math.sqrt(
        count_of_rows * lax.axis_size("lat") * column_count * lax.axis_size("lon")
    )
    mask_float = land_mask.astype(jnp.float32)[None]
    masked = ocean_state * land_mask.astype(jnp.bfloat16)[None]
    state_pad = extend(masked)
    forward = jnp.zeros((channels_per_shard, count_of_rows, column_count), jnp.float32)
    for row_offset in range(3):
        for column_offset in range(3):
            kernel_window = state_pad[
                :,
                DILATION_STEP * row_offset : DILATION_STEP * row_offset + count_of_rows,
                DILATION_STEP * column_offset : DILATION_STEP * column_offset + column_count,
            ]
            forward = forward + depth_kernel[row_offset, column_offset][
                :, None, None
            ] * kernel_window.astype(jnp.float32)
    conv_out = forward.astype(jnp.bfloat16)
    swath = (
        jnp.zeros((cells,), jnp.float32).at[swath_offset.reshape(-1)].add(swath_value.reshape(-1))
    )
    first_group = jnp.where(lax.axis_index("ch") == 0, 1.0, 0.0).astype(jnp.float32)
    cotan = (
        out_grad.astype(jnp.float32)
        .at[0]
        .add(first_group * swath.reshape(count_of_rows, column_count))
    )
    cotan = (cotan * mask_float).astype(jnp.bfloat16)
    conv_all, cotan_all = (
        lax.all_gather(conv_out, "ch", axis=0, tiled=True),
        lax.all_gather(cotan, "ch", axis=0, tiled=True),
    )
    conv_flat = conv_all.reshape(conv_all.shape[0], cells)
    cotan_flat = cotan_all.reshape(cotan_all.shape[0], cells)
    hidden = (
        jnp.dot(expand_weight.T, conv_flat, preferred_element_type=jnp.float32)
        + expand_bias[:, None]
    )
    activ, gelu_back = jax.vjp(jax.nn.gelu, hidden)
    act_grad = jnp.dot(project_weight, cotan_flat, preferred_element_type=jnp.float32)
    pre_grad = gelu_back(act_grad)[0].astype(jnp.bfloat16)
    project_part = (
        jnp.dot(activ.astype(jnp.bfloat16), cotan_flat.T, preferred_element_type=jnp.float32)
        * scale
    )
    expand_part = jnp.dot(conv_flat, pre_grad.T, preferred_element_type=jnp.float32) * scale
    bias_part = jnp.sum(pre_grad.astype(jnp.float32), axis=1) * scale
    summed = lax.psum_scatter(
        jnp.dot(expand_weight, pre_grad, preferred_element_type=jnp.float32).astype(jnp.bfloat16),
        "ch",
        scatter_dimension=0,
        tiled=True,
    )
    conv_grad = summed.reshape(channels_per_shard, count_of_rows, column_count)
    grad_pad = extend(conv_grad)
    grad_float = conv_grad.astype(jnp.float32)
    kernel_rows = []
    swapped_axes = jnp.zeros((channels_per_shard, count_of_rows, column_count), jnp.float32)
    for row_offset in range(3):
        kernel_cols = []
        for column_offset in range(3):
            kernel_window = state_pad[
                :,
                DILATION_STEP * row_offset : DILATION_STEP * row_offset + count_of_rows,
                DILATION_STEP * column_offset : DILATION_STEP * column_offset + column_count,
            ]
            kernel_cols.append(jnp.sum(grad_float * kernel_window.astype(jnp.float32), axis=(1, 2)))
            reverse_row = DILATION_STEP * (2 - row_offset)
            reverse_column = DILATION_STEP * (2 - column_offset)
            back_window = grad_pad[
                :,
                reverse_row : reverse_row + count_of_rows,
                reverse_column : reverse_column + column_count,
            ]
            swapped_axes = swapped_axes + depth_kernel[row_offset, column_offset][
                :, None, None
            ] * back_window.astype(jnp.float32)
        kernel_rows.append(jnp.stack(kernel_cols, axis=0))
    kernel_part = jnp.stack(kernel_rows, axis=0) * scale
    fold_adjustment = jnp.zeros((channels_per_shard, DILATION_STEP, column_count), jnp.float32)
    for column_offset in range(3):
        reverse_column = DILATION_STEP * (2 - column_offset)
        rim_window = grad_pad[
            :,
            count_of_rows + DILATION_STEP : count_of_rows + 2 * DILATION_STEP,
            reverse_column : reverse_column + column_count,
        ]
        weight_change = depth_kernel[2, 2 - column_offset] - depth_kernel[0, column_offset]
        fold_adjustment = fold_adjustment + weight_change[:, None, None] * rim_window.astype(
            jnp.float32
        )
    at_top = lax.axis_index("lat") == lax.axis_size("lat") - 1
    swapped_axes = swapped_axes.at[:, count_of_rows - DILATION_STEP :, :].add(
        jnp.where(at_top, fold_adjustment, jnp.zeros_like(fold_adjustment))
    )
    state_grad = (mask_float * (cotan.astype(jnp.float32) + swapped_axes)).astype(jnp.bfloat16)
    expand_grad, project_grad, bias_grad, kernel_grad = lax.psum(
        (expand_part, project_part, bias_part, kernel_part), ("lon", "lat")
    )
    return (state_grad, expand_grad, project_grad, bias_grad, kernel_grad)


def solution(mesh):
    return jax.shard_map(
        on_device,
        mesh=mesh,
        in_specs=(
            P("ch", "lat", "lon"),
            P("lat", "lon"),
            P("ch", "lat", "lon"),
            P("lat", "lon", None),
            P("lat", "lon", None),
            P(None, None, "ch"),
            P(None, "ch"),
            P("ch"),
            P("ch", None),
        ),
        out_specs=(
            P("ch", "lat", "lon"),
            P(None, "ch"),
            P("ch", None),
            P("ch"),
            P(None, None, "ch"),
        ),
        check_vma=False,
    )
```

profile of v0, /device:TPU:4, one launch (start us, length us, event | category | flops | bytes accessed | tf_op | source)
XLA Modules:
  0.0 1292.7 jit_solution(13573045520863102719)
XLA Ops:
  8.7 1.2 convert_element_type.110
  10.0 3.4 scatter_custom_fusion
  16.0 11.4 collective-permute-start.1
  28.2 1.9 collective-permute-start
  30.1 32.5 %all_gather.13 = bf16[75,2,2048]{2,1,0:T(2,128)(2,1)S(1)} all-gather(bf16[75,2,128]{2,1,0:T(2,128)(2,1)S(1)} %slice.277), channel_id=1, replica_groups=mesh['lon'=16,'lat'=8,'ch'=4] {'lon'}, dimensions={2}, use_global_device_ids=true | all-gather | bytes 652800 | tf_op jit(solution)/shard_map/all_gather | solution.py:29
  65.4 3.5 collective-permute-start.2
  69.5 5.5 rev.6
  75.7 4.0 concatenate.54
  79.7 4.5 collective-permute-start.3
  84.2 1.9 collective-permute-done.3
  86.1 1.1 broadcast_select_fusion.1
  87.2 2.4 maximum_maximum_fusion
  89.7 1.1 copy-done.1
  91.3 4.1 fusion.19
  95.6 1.3 dynamic-slice.20
  98.1 2.1 pad.67
  100.3 1.2 copy.42
  101.5 23.7 %all-gather.5.cloned.1.call-done = bf16[300,32,128]{2,1,0:T(8,128)(2,1)} async-done(((bf16[75,32,128]{2,1,0:T(8,128)(2,1)}), bf16[300,32,128]{2,1,0:T(8,128)(2,1)}) %all-gather.5.cloned.1.call-update) | async-done | bytes 2457616 | tf_op jit(solution)/shard_map/all_gather | solution.py:102
  125.2 2.1 pad.68
  127.3 1.2 copy.43
  129.4 1.9 fusion.34
  131.3 2.5 convert_reduce_fusion
  133.9 1.1 copy-done.11
  134.9 1.8 convolution_multiply_fusion
  136.7 2.2 fusion.2
  138.9 31.6 %fusion = bf16[80,4096]{1,0:T(8,128)(2,1)} fusion(bf16[300,4096]{1,0:T(8,128)(2,1)S(1)} %fusion.2), kind=kCustom, calls=%all-reduce-scatter | all-reduce-scatter fusion | flops 1310721 | bytes 3115008
  171.4 1.9 collective-permute-start.8
  173.9 5.3 collective-permute-done.8
  179.2 6.0 concatenate.62
  185.2 1.4 constant_dynamic-slice_fusion
  186.9 4.9 fusion.28
  192.2 34.5 %all_gather.15 = bf16[75,2,2048]{2,1,0:T(2,128)(2,1)S(1)} all-gather(bf16[75,2,128]{2,1,0:T(2,128)(2,1)S(1)} %slice.285), channel_id=1, replica_groups=mesh['lon'=16,'lat'=8,'ch'=4] {'lon'}, dimensions={2}, use_global_device_ids=true | all-gather | bytes 652800 | tf_op jit(solution)/shard_map/all_gather | solution.py:29
  228.3 3.0 collective-permute-start.5
  231.3 2.8 collective-permute-start.4
  234.4 3.8 collective-permute-done.4
  240.7 3.2 collective-permute-start.7
  244.0 5.5 rev.7
  250.1 4.0 concatenate.57
  254.2 311.0 %all-reduce.2 = (f32[150]{0:T(256)}, f32[3,3,75]{2,1,0:T(4,128)}) all-reduce(f32[150]{0:T(256)S(1)} %copy-done.33, f32[3,3,75]{2,1,0:T(4,128)S(1)} %maximum_multiply_fusion), channel_id=1, replica_groups=mesh['lon'=16,'lat'=8,'ch'=4] {'lon','lat'}, use_global_device_ids=true, to_apply=%region_5.6 | all-reduce | flops 825 | bytes 6600 | tf_op jit(solution)/shard_map/psum | solution.py:169
  565.2 1.9 collective-permute-start.6
  567.2 4.3 collective-permute-done.6
  571.5 1.1 broadcast_select_fusion
  572.6 2.4 pad_maximum_fusion.1
  575.2 3.4 fusion.24
  579.0 1.1 multiply_convert_fusion.2
  580.2 702.8 %all-reduce.6.cloned.1.call-done = (f32[300,150]{0,1:T(8,128)}, f32[150,300]{1,0:T(8,128)}) async-done(((f32[300,150]{0,1:T(8,128)}, f32[150,300]{1,0:T(8,128)}), (f32[300,150]{0,1:T(8,128)}, f32[150,300]{1,0:T(8,128)})) %all-reduce.6.cloned.1.call-update) | async-done | bytes 360016 | tf_op jit(solution)/shard_map/psum | solution.py:169
  1282.9 1.6 copy.49
  1284.6 1.6 copy.50
  (142 shorter events, 18.8 us)
Async XLA Ops:
  7.2 121.4 %copy-start = (bf16[300,150]{0,1:T(8,128)(2,1)S(1)}, bf16[300,150]{0,1:T(8,128)(2,1)}, u32[]{:S(2)}) copy-start(bf16[300,150]{0,1:T(8,128)(2,1)} %param.19) | copy-start | bytes 270004
  7.2 91.0 %all-gather.3.cloned.1.call-start = ((), (), s32[]{:S(2)}) async-start(), calls=%async_computation | async-start | bytes 3072000 | tf_op jit(solution)/shard_map/all_gather | solution.py:103
  14.4 110.8 %all-gather.5.cloned.1.call-start = ((), (), s32[]{:S(2)}) async-start(), calls=%async_computation.1 | async-start | bytes 3072000 | tf_op jit(solution)/shard_map/all_gather | solution.py:102
  16.0 47.9 %collective-permute-start.1 = (bf16[75,32,2]{0,1,2:T(8,128)(2,1)S(1)}, bf16[75,32,2]{0,1,2:T(8,128)(2,1)S(1)}, u32[]{:S(2)}, u32[]{:S(2)}) collective-permute-start(bf16[75,32,2]{0,1,2:T(8,128)(2,1)S(1)} %copy.31), channel_id=1, source_target_pairs={{32,0},{64,32},{96,64},{128,96},{160,128},{192,160},{224,192},{256... | collective-permute-start | bytes 28808 | tf_op jit(solution)/shard_map/ppermute | solution.py:19
  28.2 34.6 %collective-permute-start = (bf16[75,32,2]{0,1,2:T(8,128)(2,1)S(1)}, bf16[75,32,2]{0,1,2:T(8,128)(2,1)S(1)}, u32[]{:S(2)}, u32[]{:S(2)}) collective-permute-start(bf16[75,32,2]{0,1,2:T(8,128)(2,1)S(1)} %copy.30), channel_id=1, source_target_pairs={{0,32},{32,64},{64,96},{96,128},{128,160},{160,192},{192,224},{224... | collective-permute-start | bytes 28808 | tf_op jit(solution)/shard_map/ppermute | solution.py:16
  63.8 25.8 %copy-start.5 = (bf16[75,32,2]{2,1,0:T(8,128)(2,1)}, bf16[75,32,2]{2,1,0:T(8,128)(2,1)S(1)}, u32[]{:S(2)}) copy-start(bf16[75,32,2]{2,1,0:T(8,128)(2,1)S(1)} %copy.32) | copy-start | bytes 28804
  63.8 5.0 copy-start.13
  64.9 24.7 %copy-start.7 = (bf16[75,32,2]{2,1,0:T(8,128)(2,1)}, bf16[75,32,2]{2,1,0:T(8,128)(2,1)S(1)}, u32[]{:S(2)}) copy-start(bf16[75,32,2]{2,1,0:T(8,128)(2,1)S(1)} %copy.33) | copy-start | bytes 28804
  65.4 18.8 %collective-permute-start.2 = (bf16[75,2,132]{2,1,0:T(2,128)(2,1)S(1)}, bf16[75,2,132]{2,1,0:T(2,128)(2,1)}, u32[]{:S(2)}, u32[]{:S(2)}) collective-permute-start(bf16[75,2,132]{2,1,0:T(2,128)(2,1)S(1)} %get-tuple-element.51), channel_id=1, source_target_pairs={{0,4},{4,8},{8,12},{12,16},{16,20},{20,24},{24,28},{28,0},{1,5},{5... | collective-permute-start | bytes 118808 | tf_op jit(solution)/shard_map/ppermute | solution.py:16
  69.5 20.2 %copy-start.14 = (f32[75]{0:T(128)}, f32[75]{0:T(128)S(1)}, u32[]{:S(2)}) copy-start(f32[75]{0:T(128)S(1)} %get-tuple-element.72) | copy-start | bytes 904
  69.5 20.2 %copy-start.16 = (f32[75]{0:T(128)}, f32[75]{0:T(128)S(1)}, u32[]{:S(2)}) copy-start(f32[75]{0:T(128)S(1)} %get-tuple-element.73) | copy-start | bytes 904
  69.5 20.2 %copy-start.18 = (f32[75]{0:T(128)}, f32[75]{0:T(128)S(1)}, u32[]{:S(2)}) copy-start(f32[75]{0:T(128)S(1)} %get-tuple-element.74) | copy-start | bytes 904
  69.5 20.2 %copy-start.20 = (f32[75]{0:T(128)}, f32[75]{0:T(128)S(1)}, u32[]{:S(2)}) copy-start(f32[75]{0:T(128)S(1)} %get-tuple-element.75) | copy-start | bytes 904
  69.5 20.2 %copy-start.22 = (f32[75]{0:T(128)}, f32[75]{0:T(128)S(1)}, u32[]{:S(2)}) copy-start(f32[75]{0:T(128)S(1)} %get-tuple-element.76) | copy-start | bytes 904
  69.5 20.2 %copy-start.24 = (f32[75]{0:T(128)}, f32[75]{0:T(128)S(1)}, u32[]{:S(2)}) copy-start(f32[75]{0:T(128)S(1)} %get-tuple-element.77) | copy-start | bytes 904
  79.7 6.5 collective-permute-start.3
  87.2 4.1 copy-start.26
  87.2 4.1 copy-start.28
  87.2 4.1 copy-start.30
  95.4 1187.5 %all-reduce.6.cloned.1.call-start = ((), (), s32[]{:S(2)}) async-start(), calls=%async_computation.2 | async-start | bytes 933888 | tf_op jit(solution)/shard_map/psum | solution.py:169
  171.4 7.8 collective-permute-start.8
  173.3 13.4 %copy-start.8 = (bf16[75,32,2]{2,1,0:T(8,128)(2,1)S(1)}, bf16[75,32,2]{2,1,0:T(8,128)(2,1)}, u32[]{:S(2)}) copy-start(bf16[75,32,2]{2,1,0:T(8,128)(2,1)} %copy-done.7) | copy-start | bytes 28804
  179.2 7.5 copy-start.4
  192.1 42.1 %copy-start.34 = (f32[75]{0:T(128)S(1)}, f32[75]{0:T(128)}, u32[]{:S(2)}) copy-start(f32[75]{0:T(128)} %get-tuple-element.35) | copy-start | bytes 904
  192.1 42.1 %copy-start.35 = (f32[75]{0:T(128)S(1)}, f32[75]{0:T(128)}, u32[]{:S(2)}) copy-start(f32[75]{0:T(128)} %get-tuple-element.36) | copy-start | bytes 904
  192.1 42.1 %copy-start.36 = (f32[75]{0:T(128)S(1)}, f32[75]{0:T(128)}, u32[]{:S(2)}) copy-start(f32[75]{0:T(128)} %get-tuple-element.37) | copy-start | bytes 904
  192.1 42.1 %copy-start.37 = (f32[75]{0:T(128)S(1)}, f32[75]{0:T(128)}, u32[]{:S(2)}) copy-start(f32[75]{0:T(128)} %get-tuple-element.56) | copy-start | bytes 904
  192.1 42.1 %copy-start.38 = (f32[75]{0:T(128)S(1)}, f32[75]{0:T(128)}, u32[]{:S(2)}) copy-start(f32[75]{0:T(128)} %get-tuple-element.57) | copy-start | bytes 904
  192.1 42.1 %copy-start.39 = (f32[75]{0:T(128)S(1)}, f32[75]{0:T(128)}, u32[]{:S(2)}) copy-start(f32[75]{0:T(128)} %get-tuple-element.58) | copy-start | bytes 904
  192.1 42.1 %copy-start.43 = (f32[75]{0:T(128)S(1)}, f32[75]{0:T(128)}, u32[]{:S(2)}) copy-start(f32[75]{0:T(128)} %get-tuple-element.53) | copy-start | bytes 904
  192.2 42.1 %copy-start.44 = (f32[75]{0:T(128)S(1)}, f32[75]{0:T(128)}, u32[]{:S(2)}) copy-start(f32[75]{0:T(128)} %get-tuple-element.54) | copy-start | bytes 904
  192.2 42.1 %copy-start.45 = (f32[75]{0:T(128)S(1)}, f32[75]{0:T(128)}, u32[]{:S(2)}) copy-start(f32[75]{0:T(128)} %get-tuple-element.55) | copy-start | bytes 904
  228.3 10.9 collective-permute-start.5
  231.3 6.8 collective-permute-start.4
  240.7 326.4 %collective-permute-start.7 = (bf16[75,2,132]{2,1,0:T(2,128)(2,1)S(1)}, bf16[75,2,132]{2,1,0:T(2,128)(2,1)}, u32[]{:S(2)}, u32[]{:S(2)}) collective-permute-start(bf16[75,2,132]{2,1,0:T(2,128)(2,1)S(1)} %get-tuple-element.48), channel_id=1, source_target_pairs={{0,4},{4,8},{8,12},{12,16},{16,20},{20,24},{24,28},{28,0},{1,5},{5... | collective-permute-start | bytes 118808 | tf_op jit(solution)/shard_map/ppermute | solution.py:16
  244.0 10.2 copy-start.33
  565.2 6.3 collective-permute-start.6
  572.5 2.5 copy-start.15
  572.5 2.5 copy-start.17
  572.5 2.5 copy-start.19
  572.6 2.5 copy-start.21
  572.6 2.5 copy-start.23
  572.6 2.5 copy-start.25
  572.6 2.5 copy-start.27
  575.1 3.4 copy-start.40
  575.2 3.4 copy-start.41
  575.2 3.4 copy-start.42
  575.2 3.9 copy-start.10
  (11 other events, 18.3 us)
Sparse Core Ops, SparseCore 0:
  14.5 38.0 all-gather.2
  95.5 29.6 all-gather.4
  173.5 1109.3 all-reduce.5
where the time goes:
time: 1290 us
  waiting for transfers between devices  742 us (58%)
  blocking collectives  410 us (32%)
  local copies, waits for them, and re-layouts  52.1 us (4%)
  starting transfers between devices  34.4 us (3%)
  other arithmetic  30.2 us (2%)
  between operations  15.4 us (1%)
    psum x1, waiting for transfers between devices, on_device(): lax.psum((expand_part, project_part, bias_part, kernel_part), ('lon', 'la...  703 us
    psum x1, blocking collectives, on_device(): lax.psum((expand_part, project_part, bias_part, kernel_part), ('lon', 'la...  311 us
    all_gather x2, blocking collectives, extend(): gathered = lax.all_gather(uppermost_rows, 'lon', axis=2, tiled=True)  67 us
    unnamed x1, blocking collectives  31.6 us
  transfers between devices with their start and end apart: 12, of which 6 were waited for; matrix products, arithmetic and copies ran while one was open for 5% of the time, Pallas kernels for 0%

commit v1 on v0

--- a/solution.py
+++ b/solution.py
@@ -167,7 +167,8 @@
     )
     state_grad = (mask_float * (cotan.astype(jnp.float32) + swapped_axes)).astype(jnp.bfloat16)
     expand_grad, project_grad, bias_grad, kernel_grad = lax.psum(
-        (expand_part, project_part, bias_part, kernel_part), ("lon", "lat")
+        lax.psum((expand_part, project_part, bias_part, kernel_part), axis_name="lon"),
+        axis_name="lat",
     )
     return (state_grad, expand_grad, project_grad, bias_grad, kernel_grad)
 

time: 1290 us -> 415 us (0.32)
  waiting for transfers between devices: 742 us -> 122 us
  blocking collectives: 410 us -> 146 us
    psum x1 -> x2, waiting for transfers between devices: 703 us -> 83 us  [the longest x1 83 us: on_device(): lax.psum(lax.psum((expand_part, project_part, bias_part, kernel_part), ax...]
    psum x1 -> x2, blocking collectives: 311 us -> 47.2 us  [the longest x1 27.8 us: on_device(): lax.psum((expand_part, project_part, bias_part, kernel_part), axis_name='...]
  transfers between devices with their start and end apart: 12 -> 13, of which waited for: 6 -> 6; matrix products, arithmetic and copies ran while one was open for 5% -> 16% of each run, Pallas kernels for 0% -> 0%
where the time goes in v1:
time: 415 us; the launch traced here: 413 us
  blocking collectives  146 us (35%)
  waiting for transfers between devices  122 us (29%)
  local copies, waits for them, and re-layouts  52.1 us (13%)
  starting transfers between devices  34.9 us (8%)
  other arithmetic  33.6 us (8%)
  between operations  15.4 us (4%)
  matrix products  9.26 us (2%)
    psum x1, waiting for transfers between devices, on_device(): lax.psum(lax.psum((expand_part, project_part, bias_part, kernel_part), ax...  83 us
    all_gather x2, blocking collectives, extend(): gathered = lax.all_gather(uppermost_rows, 'lon', axis=2, tiled=True)  67.4 us
    unnamed x1, blocking collectives  31.6 us
    psum x1, blocking collectives, on_device(): lax.psum((expand_part, project_part, bias_part, kernel_part), axis_name='...  27.8 us
    all_gather x1, waiting for transfers between devices, on_device(): lax.all_gather(conv_out, 'ch', axis=0, tiled=True)  23.7 us
    unnamed x105, local copies, waits for them, and re-layouts  23.1 us
    ppermute x4, starting transfers between devices, with_halo(): lax.ppermute(lax.slice_in_dim(block, 0, width, axis=dim), axis, backward)  20.5 us
    psum x1, blocking collectives, on_device(): lax.psum(lax.psum((expand_part, project_part, bias_part, kernel_part), ax...  19.4 us
  transfers between devices with their start and end apart: 13, of which 6 were waited for; matrix products, arithmetic and copies ran while one was open for 16% of the time, Pallas kernels for 0%

profile of v1, /device:TPU:4, one launch (start us, length us, event | category | flops | bytes accessed | tf_op | source)
XLA Modules:
  0.0 413.3 jit_solution(2876506250483872609)
XLA Ops:
  8.7 1.2 convert_element_type.110
  10.0 3.4 scatter_custom_fusion
  16.0 11.4 %collective-permute-start.1 = (bf16[75,32,2]{0,1,2:T(8,128)(2,1)S(1)}, bf16[75,32,2]{0,1,2:T(8,128)(2,1)S(1)}, u32[]{:S(2)}, u32[]{:S(2)}) collective-permute-start(bf16[75,32,2]{0,1,2:T(8,128)(2,1)S(1)} %copy.31), channel_id=1, source_target_pairs={{32,0},{64,32},{96,64},{128,96},{160,128},{192,160},{224,192},{256... | collective-permute-start | bytes 28808 | tf_op jit(solution)/shard_map/ppermute | solution.py:19
  28.2 1.9 collective-permute-start
  30.1 32.5 %all_gather.13 = bf16[75,2,2048]{2,1,0:T(2,128)(2,1)S(1)} all-gather(bf16[75,2,128]{2,1,0:T(2,128)(2,1)S(1)} %slice.277), channel_id=1, replica_groups=mesh['lon'=16,'lat'=8,'ch'=4] {'lon'}, dimensions={2}, use_global_device_ids=true | all-gather | bytes 652800 | tf_op jit(solution)/shard_map/all_gather | solution.py:29
  65.4 3.5 collective-permute-start.2
  69.5 5.5 %rev.6 = bf16[75,2,2048]{2,1,0:T(2,128)(2,1)S(1)} reverse(bf16[75,2,2048]{2,1,0:T(2,128)(2,1)S(1)} %all_gather.13), dimensions={1,2} | reverse | bytes 1228800 | tf_op jit(solution)/shard_map/rev | solution.py:30
  75.7 4.0 concatenate.54
  79.7 4.5 %collective-permute-start.3 = (bf16[75,2,132]{2,1,0:T(2,128)(2,1)S(1)}, bf16[75,2,132]{2,1,0:T(2,128)(2,1)S(1)}, u32[]{:S(2)}, u32[]{:S(2)}) collective-permute-start(bf16[75,2,132]{2,1,0:T(2,128)(2,1)S(1)} %get-tuple-element.56), channel_id=1, source_target_pairs={{4,0},{8,4},{12,8},{16,12},{20,16},{24,20},{28,24},{0,28},{5,1},{9... | collective-permute-start | bytes 118808 | tf_op jit(solution)/shard_map/ppermute | solution.py:19
  84.2 1.9 collective-permute-done.3
  86.1 1.1 broadcast_select_fusion.1
  87.2 2.4 maximum_maximum_fusion
  91.3 4.1 fusion.19
  95.6 1.3 dynamic-slice.20
  98.1 2.1 pad.67
  100.3 1.2 copy.42
  101.5 23.7 %all-gather.5.cloned.1.call-done = bf16[300,32,128]{2,1,0:T(8,128)(2,1)} async-done(((bf16[75,32,128]{2,1,0:T(8,128)(2,1)}), bf16[300,32,128]{2,1,0:T(8,128)(2,1)}) %all-gather.5.cloned.1.call-update) | async-done | bytes 2457616 | tf_op jit(solution)/shard_map/all_gather | solution.py:102
  125.2 2.1 pad.68
  127.3 1.2 copy.43
  129.4 1.9 fusion.34
  131.3 2.5 convert_reduce_fusion
  134.9 1.8 convolution_multiply_fusion
  136.7 2.2 fusion.2
  138.9 31.6 %fusion = bf16[80,4096]{1,0:T(8,128)(2,1)} fusion(bf16[300,4096]{1,0:T(8,128)(2,1)S(1)} %fusion.2), kind=kCustom, calls=%all-reduce-scatter | all-reduce-scatter fusion | flops 1310721 | bytes 3115008
  171.4 1.9 collective-permute-start.8
  174.0 5.2 %collective-permute-done.8 = bf16[15,4096]{1,0:T(8,128)(2,1)S(1)} collective-permute-done((bf16[15,4096]{1,0:T(8,128)(2,1)S(1)}, bf16[15,4096]{1,0:T(8,128)(2,1)S(1)}, u32[]{:S(2)}, u32[]{:S(2)}) %collective-permute-start.8) | collective-permute-done | bytes 122912
  179.2 6.0 %concatenate.62 = bf16[95,4096]{1,0:T(8,128)(2,1)} concatenate(bf16[15,4096]{1,0:T(8,128)(2,1)S(1)} %collective-permute-done.8, bf16[80,4096]{1,0:T(8,128)(2,1)} %fusion), dimensions={0} | concatenate | bytes 1556480
  185.2 1.4 constant_dynamic-slice_fusion
  186.9 4.9 %fusion.28 = (f32[75]{0:T(128)}, f32[75]{0:T(128)}, f32[75]{0:T(128)}, f32[75]{0:T(128)}, f32[75]{0:T(128)}, /*index=5*/f32[75]{0:T(128)}, f32[75]{0:T(128)}, f32[75]{0:T(128)}, f32[75]{0:T(128)}) fusion(bf16[75,32,128]{2,1,0:T(8,128)(2,1)S(1)} %broadcast_multiply_fusion, bf16[75,32,2]{2,1,0:T(8,128)(2,1)S(1)} %copy-done.6, ...), kind=kLoop, calls=%fused_computation.58 | loop fusion | flops 10444125 | bytes 4937100 | tf_op jit(solution)/shard_map/reduce_sum | solution.py:139
  192.2 34.9 %all_gather.15 = bf16[75,2,2048]{2,1,0:T(2,128)(2,1)S(1)} all-gather(bf16[75,2,128]{2,1,0:T(2,128)(2,1)S(1)} %slice.285), channel_id=1, replica_groups=mesh['lon'=16,'lat'=8,'ch'=4] {'lon'}, dimensions={2}, use_global_device_ids=true | all-gather | bytes 652800 | tf_op jit(solution)/shard_map/all_gather | solution.py:29
  228.8 2.8 collective-permute-start.5
  231.5 3.1 collective-permute-start.4
  234.8 3.6 collective-permute-done.4
  240.9 3.7 collective-permute-start.7
  244.7 5.5 %rev.7 = bf16[75,2,2048]{2,1,0:T(2,128)(2,1)S(1)} reverse(bf16[75,2,2048]{2,1,0:T(2,128)(2,1)S(1)} %all_gather.15), dimensions={1,2} | reverse | bytes 1228800 | tf_op jit(solution)/shard_map/rev | solution.py:30
  250.8 4.0 concatenate.57
  254.8 27.8 %all-reduce.2 = (f32[150]{0:T(256)S(1)}, f32[3,3,75]{2,1,0:T(4,128)S(1)}) all-reduce(f32[150]{0:T(256)S(1)} %copy-done.33, f32[3,3,75]{2,1,0:T(4,128)S(1)} %maximum_multiply_fusion), channel_id=1, replica_groups=mesh['lon'=16,'lat'=8,'ch'=4] {'lon'}, use_global_device_ids=true, to_apply=%region_7.8 | all-reduce | flops 825 | bytes 6600 | tf_op jit(solution)/shard_map/psum | solution.py:170
  282.7 19.4 %all-reduce.4 = (f32[150]{0:T(256)}, f32[3,3,75]{2,1,0:T(4,128)}) all-reduce(f32[150]{0:T(256)S(1)} %get-tuple-element.41, f32[3,3,75]{2,1,0:T(4,128)S(1)} %get-tuple-element.42), channel_id=1, replica_groups=mesh['lon'=16,'lat'=8,'ch'=4] {'lat'}, use_global_device_ids=true, to_apply=%region_8.9 | all-reduce | flops 825 | bytes 6600 | tf_op jit(solution)/shard_map/psum | solution.py:169
  302.1 1.9 collective-permute-start.6
  304.1 4.3 %collective-permute-done.6 = bf16[75,2,132]{2,1,0:T(2,128)(2,1)S(1)} collective-permute-done((bf16[75,2,132]{2,1,0:T(2,128)(2,1)S(1)}, bf16[75,2,132]{2,1,0:T(2,128)(2,1)S(1)}, u32[]{:S(2)}, u32[]{:S(2)}) %collective-permute-start.6) | collective-permute-done | bytes 39632 | tf_op jit(solution)/shard_map/ppermute | solution.py:19
  308.4 1.1 broadcast_select_fusion
  309.5 2.4 pad_maximum_fusion.1
  312.1 4.1 fusion.24
  316.2 2.0 fusion.35
  318.2 2.3 multiply_convert_fusion.2
  320.5 83.0 %all-reduce.11.cloned.1.call-done = (f32[300,150]{0,1:T(8,128)}, f32[150,300]{1,0:T(8,128)}) async-done(((f32[300,150]{0,1:T(8,128)}, f32[150,300]{1,0:T(8,128)}), (f32[300,150]{0,1:T(8,128)}, f32[150,300]{1,0:T(8,128)})) %all-reduce.11.cloned.1.call-update) | async-done | bytes 360016 | tf_op jit(solution)/shard_map/psum | solution.py:169
  403.5 1.6 copy.51
  405.2 1.6 copy.52
  (146 shorter events, 20.5 us)
Async XLA Ops:
  7.2 121.4 %copy-start = (bf16[300,150]{0,1:T(8,128)(2,1)S(1)}, bf16[300,150]{0,1:T(8,128)(2,1)}, u32[]{:S(2)}) copy-start(bf16[300,150]{0,1:T(8,128)(2,1)} %param.19) | copy-start | bytes 270004
  7.2 91.0 %all-gather.3.cloned.1.call-start = ((), (), s32[]{:S(2)}) async-start(), calls=%async_computation | async-start | bytes 3072000 | tf_op jit(solution)/shard_map/all_gather | solution.py:103
  14.4 110.8 %all-gather.5.cloned.1.call-start = ((), (), s32[]{:S(2)}) async-start(), calls=%async_computation.1 | async-start | bytes 3072000 | tf_op jit(solution)/shard_map/all_gather | solution.py:102
  16.0 47.9 %collective-permute-start.1 = (bf16[75,32,2]{0,1,2:T(8,128)(2,1)S(1)}, bf16[75,32,2]{0,1,2:T(8,128)(2,1)S(1)}, u32[]{:S(2)}, u32[]{:S(2)}) collective-permute-start(bf16[75,32,2]{0,1,2:T(8,128)(2,1)S(1)} %copy.31), channel_id=1, source_target_pairs={{32,0},{64,32},{96,64},{128,96},{160,128},{192,160},{224,192},{256... | collective-permute-start | bytes 28808 | tf_op jit(solution)/shard_map/ppermute | solution.py:19
  28.2 34.6 %collective-permute-start = (bf16[75,32,2]{0,1,2:T(8,128)(2,1)S(1)}, bf16[75,32,2]{0,1,2:T(8,128)(2,1)S(1)}, u32[]{:S(2)}, u32[]{:S(2)}) collective-permute-start(bf16[75,32,2]{0,1,2:T(8,128)(2,1)S(1)} %copy.30), channel_id=1, source_target_pairs={{0,32},{32,64},{64,96},{96,128},{128,160},{160,192},{192,224},{224... | collective-permute-start | bytes 28808 | tf_op jit(solution)/shard_map/ppermute | solution.py:16
  63.8 25.8 %copy-start.5 = (bf16[75,32,2]{2,1,0:T(8,128)(2,1)}, bf16[75,32,2]{2,1,0:T(8,128)(2,1)S(1)}, u32[]{:S(2)}) copy-start(bf16[75,32,2]{2,1,0:T(8,128)(2,1)S(1)} %copy.32) | copy-start | bytes 28804
  63.8 5.0 %copy-start.13 = (f32[3,3,75]{2,1,0:T(4,128)S(1)}, f32[3,3,75]{2,1,0:T(4,128)}, u32[]{:S(2)}) copy-start(f32[3,3,75]{2,1,0:T(4,128)} %param.18) | copy-start | bytes 8104
  64.9 24.7 %copy-start.7 = (bf16[75,32,2]{2,1,0:T(8,128)(2,1)}, bf16[75,32,2]{2,1,0:T(8,128)(2,1)S(1)}, u32[]{:S(2)}) copy-start(bf16[75,32,2]{2,1,0:T(8,128)(2,1)S(1)} %copy.33) | copy-start | bytes 28804
  65.4 18.8 %collective-permute-start.2 = (bf16[75,2,132]{2,1,0:T(2,128)(2,1)S(1)}, bf16[75,2,132]{2,1,0:T(2,128)(2,1)}, u32[]{:S(2)}, u32[]{:S(2)}) collective-permute-start(bf16[75,2,132]{2,1,0:T(2,128)(2,1)S(1)} %get-tuple-element.55), channel_id=1, source_target_pairs={{0,4},{4,8},{8,12},{12,16},{16,20},{20,24},{24,28},{28,0},{1,5},{5... | collective-permute-start | bytes 118808 | tf_op jit(solution)/shard_map/ppermute | solution.py:16
  69.5 20.2 %copy-start.14 = (f32[75]{0:T(128)}, f32[75]{0:T(128)S(1)}, u32[]{:S(2)}) copy-start(f32[75]{0:T(128)S(1)} %get-tuple-element.76) | copy-start | bytes 904
  69.5 20.2 %copy-start.16 = (f32[75]{0:T(128)}, f32[75]{0:T(128)S(1)}, u32[]{:S(2)}) copy-start(f32[75]{0:T(128)S(1)} %get-tuple-element.77) | copy-start | bytes 904
  69.5 20.2 %copy-start.18 = (f32[75]{0:T(128)}, f32[75]{0:T(128)S(1)}, u32[]{:S(2)}) copy-start(f32[75]{0:T(128)S(1)} %get-tuple-element.78) | copy-start | bytes 904
  69.5 20.2 %copy-start.20 = (f32[75]{0:T(128)}, f32[75]{0:T(128)S(1)}, u32[]{:S(2)}) copy-start(f32[75]{0:T(128)S(1)} %get-tuple-element.79) | copy-start | bytes 904
  69.5 20.2 %copy-start.22 = (f32[75]{0:T(128)}, f32[75]{0:T(128)S(1)}, u32[]{:S(2)}) copy-start(f32[75]{0:T(128)S(1)} %get-tuple-element.80) | copy-start | bytes 904
  69.5 20.2 %copy-start.24 = (f32[75]{0:T(128)}, f32[75]{0:T(128)S(1)}, u32[]{:S(2)}) copy-start(f32[75]{0:T(128)S(1)} %get-tuple-element.81) | copy-start | bytes 904
  79.7 6.5 %collective-permute-start.3 = (bf16[75,2,132]{2,1,0:T(2,128)(2,1)S(1)}, bf16[75,2,132]{2,1,0:T(2,128)(2,1)S(1)}, u32[]{:S(2)}, u32[]{:S(2)}) collective-permute-start(bf16[75,2,132]{2,1,0:T(2,128)(2,1)S(1)} %get-tuple-element.56), channel_id=1, source_target_pairs={{4,0},{8,4},{12,8},{16,12},{20,16},{24,20},{28,24},{0,28},{5,1},{9... | collective-permute-start | bytes 118808 | tf_op jit(solution)/shard_map/ppermute | solution.py:19
  87.2 4.1 copy-start.26
  87.2 4.1 copy-start.28
  87.2 4.1 copy-start.30
  95.4 220.8 %all-reduce.9.cloned.1.call-start = ((), (), s32[]{:S(2)}) async-start(), calls=%async_computation.2 | async-start | bytes 933888 | tf_op jit(solution)/shard_map/psum | solution.py:170
  171.4 7.8 %collective-permute-start.8 = (bf16[15,4096]{1,0:T(8,128)(2,1)S(1)}, bf16[15,4096]{1,0:T(8,128)(2,1)S(1)}, u32[]{:S(2)}, u32[]{:S(2)}) collective-permute-start(bf16[15,4096]{1,0:T(8,128)(2,1)S(1)} %slice.298), channel_id=1, source_target_pairs={{0,1},{1,2},{2,3},{4,5},{5,6},{6,7},{8,9},{9,10},{10,11},{12,13},{... | collective-permute-start | bytes 368648
  173.3 13.4 %copy-start.8 = (bf16[75,32,2]{2,1,0:T(8,128)(2,1)S(1)}, bf16[75,32,2]{2,1,0:T(8,128)(2,1)}, u32[]{:S(2)}) copy-start(bf16[75,32,2]{2,1,0:T(8,128)(2,1)} %copy-done.7) | copy-start | bytes 28804
  173.4 230.1 %all-reduce.11.cloned.1.call-start = ((), (), s32[]{:S(2)}) async-start(), calls=%async_computation.3 | async-start | bytes 933888 | tf_op jit(solution)/shard_map/psum | solution.py:169
  179.2 7.5 %copy-start.4 = (bf16[75,34,132]{2,1,0:T(8,128)(2,1)S(1)}, bf16[75,34,132]{2,1,0:T(8,128)(2,1)}, u32[]{:S(2)}) copy-start(bf16[75,34,132]{2,1,0:T(8,128)(2,1)} %copy-done.3) | copy-start | bytes 2019604
  192.1 42.5 %copy-start.34 = (f32[75]{0:T(128)S(1)}, f32[75]{0:T(128)}, u32[]{:S(2)}) copy-start(f32[75]{0:T(128)} %get-tuple-element.35) | copy-start | bytes 904
  192.1 42.5 %copy-start.35 = (f32[75]{0:T(128)S(1)}, f32[75]{0:T(128)}, u32[]{:S(2)}) copy-start(f32[75]{0:T(128)} %get-tuple-element.36) | copy-start | bytes 904
  192.1 42.5 %copy-start.36 = (f32[75]{0:T(128)S(1)}, f32[75]{0:T(128)}, u32[]{:S(2)}) copy-start(f32[75]{0:T(128)} %get-tuple-element.37) | copy-start | bytes 904
  192.1 42.5 %copy-start.37 = (f32[75]{0:T(128)S(1)}, f32[75]{0:T(128)}, u32[]{:S(2)}) copy-start(f32[75]{0:T(128)} %get-tuple-element.60) | copy-start | bytes 904
  192.1 42.5 %copy-start.38 = (f32[75]{0:T(128)S(1)}, f32[75]{0:T(128)}, u32[]{:S(2)}) copy-start(f32[75]{0:T(128)} %get-tuple-element.61) | copy-start | bytes 904
  192.1 42.5 %copy-start.39 = (f32[75]{0:T(128)S(1)}, f32[75]{0:T(128)}, u32[]{:S(2)}) copy-start(f32[75]{0:T(128)} %get-tuple-element.62) | copy-start | bytes 904
  192.1 42.5 %copy-start.43 = (f32[75]{0:T(128)S(1)}, f32[75]{0:T(128)}, u32[]{:S(2)}) copy-start(f32[75]{0:T(128)} %get-tuple-element.57) | copy-start | bytes 904
  192.2 42.5 %copy-start.44 = (f32[75]{0:T(128)S(1)}, f32[75]{0:T(128)}, u32[]{:S(2)}) copy-start(f32[75]{0:T(128)} %get-tuple-element.58) | copy-start | bytes 904
  192.2 42.5 %copy-start.45 = (f32[75]{0:T(128)S(1)}, f32[75]{0:T(128)}, u32[]{:S(2)}) copy-start(f32[75]{0:T(128)} %get-tuple-element.59) | copy-start | bytes 904
  228.8 10.7 %collective-permute-start.5 = (bf16[75,32,2]{0,1,2:T(8,128)(2,1)S(1)}, bf16[75,32,2]{0,1,2:T(8,128)(2,1)S(1)}, u32[]{:S(2)}, u32[]{:S(2)}) collective-permute-start(bf16[75,32,2]{0,1,2:T(8,128)(2,1)S(1)} %copy.37), channel_id=1, source_target_pairs={{32,0},{64,32},{96,64},{128,96},{160,128},{192,160},{224,192},{256... | collective-permute-start | bytes 28808 | tf_op jit(solution)/shard_map/ppermute | solution.py:19
  231.5 6.8 %collective-permute-start.4 = (bf16[75,32,2]{0,1,2:T(8,128)(2,1)S(1)}, bf16[75,32,2]{0,1,2:T(8,128)(2,1)S(1)}, u32[]{:S(2)}, u32[]{:S(2)}) collective-permute-start(bf16[75,32,2]{0,1,2:T(8,128)(2,1)S(1)} %copy.36), channel_id=1, source_target_pairs={{0,32},{32,64},{64,96},{96,128},{128,160},{160,192},{192,224},{224... | collective-permute-start | bytes 28808 | tf_op jit(solution)/shard_map/ppermute | solution.py:16
  240.9 63.1 %collective-permute-start.7 = (bf16[75,2,132]{2,1,0:T(2,128)(2,1)S(1)}, bf16[75,2,132]{2,1,0:T(2,128)(2,1)}, u32[]{:S(2)}, u32[]{:S(2)}) collective-permute-start(bf16[75,2,132]{2,1,0:T(2,128)(2,1)S(1)} %get-tuple-element.52), channel_id=1, source_target_pairs={{0,4},{4,8},{8,12},{12,16},{16,20},{20,24},{24,28},{28,0},{1,5},{5... | collective-permute-start | bytes 118808 | tf_op jit(solution)/shard_map/ppermute | solution.py:16
  244.6 10.2 %copy-start.33 = (f32[150]{0:T(256)S(1)}, f32[150]{0:T(256)}, u32[]{:S(2)}) copy-start(f32[150]{0:T(256)} %broadcast_multiply_fusion.1) | copy-start | bytes 1804
  302.1 6.3 %collective-permute-start.6 = (bf16[75,2,132]{2,1,0:T(2,128)(2,1)S(1)}, bf16[75,2,132]{2,1,0:T(2,128)(2,1)S(1)}, u32[]{:S(2)}, u32[]{:S(2)}) collective-permute-start(bf16[75,2,132]{2,1,0:T(2,128)(2,1)S(1)} %get-tuple-element.51), channel_id=1, source_target_pairs={{4,0},{8,4},{12,8},{16,12},{20,16},{24,20},{28,24},{0,28},{5,1},{9... | collective-permute-start | bytes 118808 | tf_op jit(solution)/shard_map/ppermute | solution.py:19
  309.4 2.5 copy-start.15
  309.4 2.5 copy-start.17
  309.4 2.5 copy-start.19
  309.4 2.5 copy-start.21
  309.5 2.5 copy-start.23
  309.5 2.5 copy-start.25
  312.0 4.2 %copy-start.40 = (f32[75]{0:T(128)S(1)}, f32[75]{0:T(128)}, u32[]{:S(2)}) copy-start(f32[75]{0:T(128)} %get-tuple-element.73) | copy-start | bytes 904
  312.0 4.2 %copy-start.41 = (f32[75]{0:T(128)S(1)}, f32[75]{0:T(128)}, u32[]{:S(2)}) copy-start(f32[75]{0:T(128)} %get-tuple-element.74) | copy-start | bytes 904
  312.1 4.2 %copy-start.42 = (f32[75]{0:T(128)S(1)}, f32[75]{0:T(128)}, u32[]{:S(2)}) copy-start(f32[75]{0:T(128)} %get-tuple-element.75) | copy-start | bytes 904
  312.1 6.2 %copy-start.10 = (f32[75,32,128]{2,1,0:T(8,128)S(1)}, f32[75,32,128]{2,1,0:T(8,128)}, u32[]{:S(2)}) copy-start(f32[75,32,128]{2,1,0:T(8,128)} %copy-done.9) | copy-start | bytes 3686404
  (12 other events, 20.8 us)
Sparse Core Ops, SparseCore 0:
  14.5 38.0 all-gather.2
  95.5 29.6 all-gather.4
  173.5 138.7 all-reduce.8
  316.3 87.1 all-reduce.10
